TPU v7x, 32 devices: a whole 2x2x4 slice. The times are simulated.
32 devices in a mesh: groups: 2 (over x), tm: 16 (over z, y, core).
Axes of the slice: x: 2, y: 2, z: 4, core: 2. Of those that a mesh axis runs over, the one named last changes fastest.
Arguments:
- space_time: bfloat16 [32, 512, 1024], P(('groups', 'tm')), parts along dimension 0, may hold values from -16 to 16
- w_lin: bfloat16 [1024, 3072], replicated, may hold values from -0.1875 to 0.1875
- gain_lin: bfloat16 [1024], replicated, may hold values from 0.099609375 to 1.8984375
- w_query: bfloat16 [1024, 1024], replicated, may hold values from -4 to 4
- w_kv: bfloat16 [1024, 512], replicated, may hold values from -4 to 4
- frame_attention_gain: bfloat16 [1024], replicated, may hold values from 0.099609375 to 1.8984375
Outputs:
- attended: bfloat16 [32, 512, 1024], P(('groups', 'tm')), parts along dimension 0
There are 2 independent parts, one for each index of `groups`. A program takes and returns all parts, laid end to end along the dimension named above; an argument that names none is the same for every part. Nothing has to cross between parts.
All inputs are finite; a program needn't handle non-finite values.
Results may differ from a plain program's by a relative error of at most 0.028.
The roundings to bfloat16 on the way count: a program that leaves them out, or rounds other values in their place, can miss the bound.
Values may be sent and summed in bfloat16 or wider, within the bound.
A program may use at most 64 MiB of HBM per device.

v0:
```python
import functools
import math

import jax
import jax.numpy as jnp
from jax import lax
from jax.experimental import pallas as pl
from jax.experimental.pallas import tpu as pltpu
from jax.sharding import PartitionSpec as P

HEADS = 8
HD = 128
KVH = 2
P_SIZE = 512
SB = 16
SPAN = 128
PAIR = 2 * HD
STAGES = HEADS // 2
TOKENS = P_SIZE // SB
QUARTERS = 4
ROWS_Q = P_SIZE // QUARTERS

epsilon = 1e-06


def shifted(block, axis, distance):
    devices = range(lax.axis_size(axis))
    route = [(i - distance, i) for i in devices if i - distance in devices]
    return lax.ppermute(block, axis, route)


def carried_state(tokens, w_lin, count):
    width = tokens.shape[1]
    rows = tokens.shape[0]
    packed = jnp.dot(tokens, w_lin[:, width:], preferred_element_type=jnp.float32).astype(jnp.bfloat16)
    keys = packed[:, :width].reshape(rows, HEADS, HD)
    values = packed[:, width:].reshape(rows, HEADS, HD)
    total = jnp.einsum("nhd,nhe->hde", keys, values, preferred_element_type=jnp.float32)
    within = lax.axis_index("tm") // SB

    def hop(_, state):
        return jnp.where(within > 0, shifted(state + total, "tm", SB), 0.0)

    return lax.fori_loop(0, count // SB - 1, hop, jnp.zeros_like(total))


def dot(a, b):
    return jnp.dot(a, b, preferred_element_type=jnp.float32)


def dot_t(a, b):
    return lax.dot_general(a, b, (((1,), (1,)), ((), ())), preferred_element_type=jnp.float32)


def t_dot(a, b):
    return lax.dot_general(a, b, (((0,), (0,)), ((), ())), preferred_element_type=jnp.float32)


def kernel(count, *refs):
    long = count > SB
    tokens_hbm, w_lin_hbm, gain_lin, w_query_hbm, w_kv_hbm, gain_frame = refs[:6]
    refs = refs[6:]
    if long:
        incoming = refs[0]
        refs = refs[1:]
    (out_hbm, tokens, w_buf, wq_buf, wkv_buf, gains, qkv, hid, recv, normed, kv_own, kv_prev, queries, o_own, m_own,
     l_own, out_s, in_sem, w_sem, send_sem, recv_sem, kv_send, kv_recv, out_sem) = refs
    width = tokens.shape[1]
    rows = tokens.shape[0]

    me = lax.axis_index("tm")
    position = lax.rem(me, SB)
    base = me - position
    bits = [lax.rem(position // (1 << i), 2) for i in range(4)]

    def partner(j):
        return sum(lax.rem(bits[i] + ((j >> i) & 1), 2) * (1 << i) for i in range(4))

    last = me == count - 1
    barrier = pltpu.get_barrier_semaphore()

    token_copy = pltpu.make_async_copy(tokens_hbm.at[0], tokens, in_sem.at[0])
    token_copy.start()

    def w_copy(stage, c):
        start = c * width + stage * PAIR
        if not isinstance(stage, int):
            start = pl.multiple_of(start, PAIR)
        return pltpu.make_async_copy(
            w_lin_hbm.at[:, pl.ds(start, PAIR)], w_buf.at[stage, c], w_sem.at[stage, c]
        )

    for c in range(3):
        w_copy(0, c).start()
    wkv_copy = pltpu.make_async_copy(w_kv_hbm, wkv_buf, in_sem.at[1])
    wq_copy = pltpu.make_async_copy(w_query_hbm, wq_buf, in_sem.at[2])

    beside, near, across = [1, 2, 3], [4, 5, 6, 7], list(range(8, SB))
    peers = across + near + beside
    for j in peers:
        pl.semaphore_signal(barrier, inc=1, device_id={"tm": base + partner(j)})
    if long:
        @pl.when(jnp.logical_and(position == SB - 1, jnp.logical_not(last)))
        def _():
            pl.semaphore_signal(barrier, inc=1, device_id={"tm": me + 1})

        @pl.when(jnp.logical_and(position == 0, me > 0))
        def _():
            pl.semaphore_signal(barrier, inc=1, device_id={"tm": me - 1})

    line = gain_lin[...].astype(jnp.float32).reshape(1, width)
    frame = gain_frame[...].astype(jnp.float32).reshape(1, width)
    for stage in range(STAGES):
        gains[stage] = line[:, stage * PAIR:(stage + 1) * PAIR]
        gains[STAGES + stage] = frame[:, stage * PAIR:(stage + 1) * PAIR]

    causal = lax.broadcasted_iota(jnp.int32, (SPAN, SPAN), 0) >= lax.broadcasted_iota(jnp.int32, (SPAN, SPAN), 1)

    def piece(stage, j):
        other = partner(j)
        return pltpu.make_async_remote_copy(
            src_ref=hid.at[stage, pl.ds(pl.multiple_of(other * TOKENS, TOKENS), TOKENS)],
            dst_ref=recv.at[stage, pl.ds(pl.multiple_of(position * TOKENS, TOKENS), TOKENS)],
            send_sem=send_sem.at[stage, j],
            recv_sem=recv_sem.at[stage, position],
            device_id={"tm": base + other},
        )

    def arrival(stage, j):
        other = partner(j)
        return pltpu.make_async_remote_copy(
            src_ref=hid.at[stage, pl.ds(pl.multiple_of(position * TOKENS, TOKENS), TOKENS)],
            dst_ref=recv.at[stage, pl.ds(pl.multiple_of(other * TOKENS, TOKENS), TOKENS)],
            send_sem=send_sem.at[stage, j],
            recv_sem=recv_sem.at[stage, other],
            device_id={"tm": base + other},
        )

    token_copy.wait()

    def mix(stage, _):
        for c in range(3):
            w_copy(stage, c).wait()

        @pl.when(stage + 1 < STAGES)
        def _():
            for c in range(3):
                w_copy(stage + 1, c).start()

        @pl.when(stage + 1 == STAGES)
        def _():
            wkv_copy.start()
            wq_copy.start()

        for c in range(3):
            qkv[c] = dot(tokens[...], w_buf[stage, c]).astype(jnp.bfloat16)
        for half in range(2):
            columns = slice(half * HD, (half + 1) * HD)
            if long:
                state = incoming[2 * stage + half]
            else:
                state = jnp.zeros((HD, HD), jnp.float32)
            gain = gains[stage][:, columns]
            wide = pl.ds(pl.multiple_of(stage * PAIR + half * HD, HD), HD)
            for b in range(rows // SPAN):
                span = slice(b * SPAN, (b + 1) * SPAN)
                q, k, v = qkv[0, span, columns], qkv[1, span, columns], qkv[2, span, columns]
                local = jnp.where(causal, dot_t(q, k), 0.0).astype(jnp.bfloat16)
                if b == 0 and not long:
                    mixed = dot(local, v)
                else:
                    mixed = dot(
                        jnp.concatenate([q, local], axis=1),
                        jnp.concatenate([state.astype(jnp.bfloat16), v], axis=0),
                    )
                if b + 1 < rows // SPAN:
                    state = state + t_dot(k, v)
                mean = jnp.mean(mixed * mixed, axis=-1, keepdims=True)
                grown = mixed * lax.rsqrt(mean + epsilon) * gain
                hid[stage, span, columns] = (tokens[span, wide].astype(jnp.float32) + grown).astype(jnp.bfloat16)

        @pl.when(stage == 0)
        def _():
            extra = 0
            if long:
                extra = (
                    jnp.logical_and(position == SB - 1, jnp.logical_not(last)).astype(jnp.int32)
                    + jnp.logical_and(position == 0, me > 0).astype(jnp.int32)
                )
            pl.semaphore_wait(barrier, SB - 1 + extra)

        for j in near + across[:4] + beside:
            piece(stage, j).start()

        @pl.when(stage < STAGES - 2)
        def _():
            for j in across[4:]:
                piece(stage, j).start()

        @pl.when(stage == STAGES - 1)
        def _():
            for late in range(STAGES - 2, STAGES):
                for j in across[4:]:
                    piece(late, j).start()

        mine = pl.ds(pl.multiple_of(position * TOKENS, TOKENS), TOKENS)
        recv[stage, mine] = hid[stage, mine]
        return 0

    lax.fori_loop(0, STAGES, mix, 0)

    def kv_copy(block, device):
        return pltpu.make_async_remote_copy(
            src_ref=kv_own.at[:, block], dst_ref=kv_prev.at[:, block], send_sem=kv_send.at[block],
            recv_sem=kv_recv.at[block], device_id={"tm": device},
        )

    wkv_copy.wait()
    wq_copy.wait()
    for group in range(QUARTERS):
        for stage in range(STAGES):
            for j in range(4 * group, 4 * group + 4):
                if j:
                    arrival(stage, j).wait_recv()
        block = sum(lax.rem(bits[i + 2] + ((group >> i) & 1), 2) * (1 << i) for i in range(2))
        span = pl.ds(pl.multiple_of(block * ROWS_Q, ROWS_Q), ROWS_Q)
        parts = [recv[stage, span].astype(jnp.float32) for stage in range(STAGES)]
        mean = sum(jnp.sum(p * p, axis=-1, keepdims=True) for p in parts) / width
        inverse = lax.rsqrt(mean + epsilon)
        for stage in range(STAGES):
            normed[:, stage * PAIR:(stage + 1) * PAIR] = (
                parts[stage] * inverse * gains[STAGES + stage]
            ).astype(jnp.bfloat16)
        pairs = dot(normed[...], wkv_buf[...])
        for i in range(KVH):
            kv_own[i, block] = pairs[:, i * HD:(i + 1) * HD].astype(jnp.bfloat16)
            values = pairs[:, (KVH + i) * HD:(KVH + i + 1) * HD]
            kv_own[KVH + i, block] = values.T.astype(jnp.bfloat16)

        @pl.when(jnp.logical_not(last))
        def _():
            kv_copy(block, me + 1).start()

        for step in range(STAGES):
            q_pair = dot(normed[...], wq_buf[:, step * PAIR:(step + 1) * PAIR]).astype(jnp.bfloat16)
            for half in range(2):
                queries[2 * step + half, span] = q_pair[:, half * HD:(half + 1) * HD]

    factor = math.log2(math.e) / math.sqrt(HD)
    sharing = HEADS // KVH

    def keys_of(ref, kv_head):
        return ref[kv_head].reshape(P_SIZE, HD)

    def values_of(ref, kv_head):
        return jnp.concatenate([ref[KVH + kv_head, b] for b in range(QUARTERS)], axis=1)

    def own(kv_head, _):
        keys, values = keys_of(kv_own, kv_head), values_of(kv_own, kv_head)
        for g in range(sharing):
            head = kv_head * sharing + g
            s = dot_t(keys, queries[head])
            m = jnp.max(s, axis=0, keepdims=True)
            p = jnp.exp2((s - m) * factor)
            m_own[head] = m
            l_own[head] = jnp.sum(p, axis=0, keepdims=True)
            o_own[head] = dot(values, p.astype(jnp.bfloat16))
        return 0

    lax.fori_loop(0, KVH, own, 0)

    def out_copy(step):
        start = step * HD
        if not isinstance(step, int):
            start = pl.multiple_of(start, HD)
        return pltpu.make_async_copy(out_s.at[step], out_hbm.at[0, :, pl.ds(start, HD)], out_sem.at[step])

    @pl.when(me > 0)
    def _():
        for block in range(QUARTERS):
            kv_copy(block, me - 1).wait_recv()

        def earlier(kv_head, _):
            keys, values = keys_of(kv_prev, kv_head), values_of(kv_prev, kv_head)
            for g in range(sharing):
                head = kv_head * sharing + g
                s = dot_t(keys, queries[head])
                m = jnp.maximum(jnp.max(s, axis=0, keepdims=True), m_own[head])
                p = jnp.exp2((s - m) * factor)
                scale = jnp.exp2((m_own[head] - m) * factor)
                total = jnp.sum(p, axis=0, keepdims=True) + l_own[head] * scale
                o = dot(values, p.astype(jnp.bfloat16)) + o_own[head] * scale
                out_s[head] = (o / total).T.astype(jnp.bfloat16)
                out_copy(head).start()
            return 0

        lax.fori_loop(0, KVH, earlier, 0)

    @pl.when(me == 0)
    def _():
        def alone(head, _):
            out_s[head] = (o_own[head] / l_own[head]).T.astype(jnp.bfloat16)
            out_copy(head).start()
            return 0

        lax.fori_loop(0, HEADS, alone, 0)

    def sent(stage, _):
        for j in peers:
            piece(stage, j).wait_send()
        return 0

    lax.fori_loop(0, STAGES, sent, 0)

    @pl.when(jnp.logical_not(last))
    def _():
        for block in range(QUARTERS):
            kv_copy(block, me + 1).wait_send()

    for step in range(HEADS):
        out_copy(step).wait()


def body(count, space_time, w_lin, gain_lin, w_query, w_kv, frame_attention_gain):
    rows, width = space_time.shape[1:]
    args = [space_time, w_lin, gain_lin, w_query, w_kv, frame_attention_gain]
    hbm = pl.BlockSpec(memory_space=pl.ANY)
    vmem = pl.BlockSpec(memory_space=pltpu.VMEM)
    specs = [hbm, hbm, vmem, hbm, hbm, vmem]
    if count > SB:
        args.append(carried_state(space_time[0], w_lin, count))
        specs.append(vmem)
    bf16, f32 = jnp.bfloat16, jnp.float32
    return pl.pallas_call(
        functools.partial(kernel, count),
        out_shape=jax.ShapeDtypeStruct(space_time.shape, bf16),
        in_specs=specs,
        out_specs=hbm,
        scratch_shapes=[
            pltpu.VMEM((rows, width), bf16),
            pltpu.VMEM((STAGES, 3, width, PAIR), bf16),
            pltpu.VMEM(w_query.shape, bf16),
            pltpu.VMEM(w_kv.shape, bf16),
            pltpu.VMEM((2 * STAGES, 1, PAIR), f32),
            pltpu.VMEM((3, rows, PAIR), bf16),
            pltpu.VMEM((STAGES, rows, PAIR), bf16),
            pltpu.VMEM((STAGES, P_SIZE, PAIR), bf16),
            pltpu.VMEM((ROWS_Q, width), bf16),
            pltpu.VMEM((2 * KVH, QUARTERS, ROWS_Q, HD), bf16),
            pltpu.VMEM((2 * KVH, QUARTERS, ROWS_Q, HD), bf16),
            pltpu.VMEM((HEADS, P_SIZE, HD), bf16),
            pltpu.VMEM((HEADS, HD, P_SIZE), f32),
            pltpu.VMEM((HEADS, 1, P_SIZE), f32),
            pltpu.VMEM((HEADS, 1, P_SIZE), f32),
            pltpu.VMEM((HEADS, P_SIZE, HD), bf16),
            pltpu.SemaphoreType.DMA((3,)),
            pltpu.SemaphoreType.DMA((STAGES, 3)),
            pltpu.SemaphoreType.DMA((STAGES, SB)),
            pltpu.SemaphoreType.DMA((STAGES, SB)),
            pltpu.SemaphoreType.DMA((QUARTERS,)),
            pltpu.SemaphoreType.DMA((QUARTERS,)),
            pltpu.SemaphoreType.DMA((HEADS,)),
        ],
        compiler_params=pltpu.CompilerParams(
            collective_id=0, has_side_effects=True, vmem_limit_bytes=60 * 1024 * 1024
        ),
        name="video_layer",
    )(*args)


def solution(mesh):
    placed = (P(("groups", "tm"), None, None), P(), P(), P(), P(), P())
    return jax.shard_map(
        functools.partial(body, mesh.shape["tm"]),
        mesh=mesh,
        in_specs=placed,
        out_specs=P(("groups", "tm"), None, None),
        check_vma=False,
    )
```

profile of v0, /device:TPU:1, one launch (start us, length us, event | category | flops | bytes accessed | tf_op | source)
XLA Modules:
  0.0 45.8 jit_solution(6934222185285308600)
XLA Ops:
  0.0 43.6 %video_layer.1 = bf16[1,512,1024]{2,1,0:T(8,128)(2,1)} custom-call(bf16[1,512,1024]{2,1,0:T(8,128)(2,1)} %refs_0_.1, bf16[1024,3072]{1,0:T(8,128)(2,1)} %refs_1_.1, bf16[1024]{0:T(1024)(128)(2,1)} %refs_2_.1, bf16[1024,1024]{1,0:T(8,128)(2,1)} %refs_3_.1, bf16[1024,512]{1,0:T(8,128)(2,1)} %refs_4_.1, bf16[1024]{0:T(1024)(128)(2,1)} %refs_5_.1), custom_call_target="tpu_custom_call" | custom-call | tf_op jit(solution)/shard_map/video_layer/pallas_call | solution.py:334
  43.6 2.3 %copy.8 = bf16[1,512,1024]{2,1,0:T(8,128)(2,1)} copy(bf16[1,512,1024]{2,1,0:T(8,128)(2,1)} %video_layer.1) | data formatting | bytes 2097152
where the time goes:
time: 46.1 us; the launch traced here: 45.8 us
  Pallas kernels  43.6 us (95%)
  local copies, waits for them, and re-layouts  2.26 us (5%)
    pallas_call x1, Pallas kernels, body(): pl.pallas_call(functools.partial(kernel, count), out_shape=jax.ShapeDtype...  43.6 us
    unnamed x1, local copies, waits for them, and re-layouts  2.26 us

commit v1 on v0

--- a/solution.py
+++ b/solution.py
@@ -19,6 +19,7 @@
 TOKENS = P_SIZE // SB
 QUARTERS = 4
 ROWS_Q = P_SIZE // QUARTERS
+CHUNKS = [(0, 2), (2, 1), (3, 1)]
 
 epsilon = 1e-06
 
@@ -63,8 +64,8 @@
     if long:
         incoming = refs[0]
         refs = refs[1:]
-    (out_hbm, tokens, w_buf, wq_buf, wkv_buf, gains, qkv, hid, recv, normed, kv_own, kv_prev, queries, o_own, m_own,
-     l_own, out_s, in_sem, w_sem, send_sem, recv_sem, kv_send, kv_recv, out_sem) = refs
+    (out_s, tokens, w_buf, wq_buf, wkv_buf, gains, qkv, hid, recv, normed, kv_own, kv_prev, queries, o_run, m_run,
+     l_run, in_sem, w_sem, send_sem, recv_sem, kv_send, kv_recv) = refs
     width = tokens.shape[1]
     rows = tokens.shape[0]
 
@@ -192,118 +193,144 @@
         for j in near + across[:4] + beside:
             piece(stage, j).start()
 
-        @pl.when(stage < STAGES - 2)
-        def _():
-            for j in across[4:]:
-                piece(stage, j).start()
-
-        @pl.when(stage == STAGES - 1)
-        def _():
-            for late in range(STAGES - 2, STAGES):
-                for j in across[4:]:
-                    piece(late, j).start()
-
         mine = pl.ds(pl.multiple_of(position * TOKENS, TOKENS), TOKENS)
         recv[stage, mine] = hid[stage, mine]
         return 0
 
     lax.fori_loop(0, STAGES, mix, 0)
 
-    def kv_copy(block, device):
+    for j in across[4:]:
+        for stage in range(STAGES):
+            piece(stage, j).start()
+
+    def kv_copy(chunk, device):
+        first, blocks = CHUNKS[chunk]
         return pltpu.make_async_remote_copy(
-            src_ref=kv_own.at[:, block], dst_ref=kv_prev.at[:, block], send_sem=kv_send.at[block],
-            recv_sem=kv_recv.at[block], device_id={"tm": device},
+            src_ref=kv_own.at[:, pl.ds(first, blocks)], dst_ref=kv_prev.at[:, pl.ds(first, blocks)],
+            send_sem=kv_send.at[chunk], recv_sem=kv_recv.at[chunk], device_id={"tm": device},
         )
+
+    def kv_twice(chunk):
+        first, blocks = CHUNKS[chunk]
+        return pltpu.make_async_copy(
+            kv_own.at[:, pl.ds(first, blocks)], kv_prev.at[:, pl.ds(first, blocks)], kv_recv.at[chunk]
+        )
+
+    def place(first, blocks):
+        block = sum(lax.rem(bits[i + 2] + ((first >> i) & 1), 2) * (1 << i) for i in range(2))
+        block = block // blocks * blocks
+        return pl.ds(pl.multiple_of(block * ROWS_Q, blocks * ROWS_Q), blocks * ROWS_Q)
 
     wkv_copy.wait()
     wq_copy.wait()
-    for group in range(QUARTERS):
+
+    def project(chunk):
+        first, blocks = CHUNKS[chunk]
+        count_rows = blocks * ROWS_Q
         for stage in range(STAGES):
-            for j in range(4 * group, 4 * group + 4):
+            for j in range(4 * first, 4 * (first + blocks)):
                 if j:
                     arrival(stage, j).wait_recv()
-        block = sum(lax.rem(bits[i + 2] + ((group >> i) & 1), 2) * (1 << i) for i in range(2))
-        span = pl.ds(pl.multiple_of(block * ROWS_Q, ROWS_Q), ROWS_Q)
+        span = place(first, blocks)
         parts = [recv[stage, span].astype(jnp.float32) for stage in range(STAGES)]
         mean = sum(jnp.sum(p * p, axis=-1, keepdims=True) for p in parts) / width
         inverse = lax.rsqrt(mean + epsilon)
         for stage in range(STAGES):
-            normed[:, stage * PAIR:(stage + 1) * PAIR] = (
+            normed[:count_rows, stage * PAIR:(stage + 1) * PAIR] = (
                 parts[stage] * inverse * gains[STAGES + stage]
             ).astype(jnp.bfloat16)
-        pairs = dot(normed[...], wkv_buf[...])
-        for i in range(KVH):
-            kv_own[i, block] = pairs[:, i * HD:(i + 1) * HD].astype(jnp.bfloat16)
-            values = pairs[:, (KVH + i) * HD:(KVH + i + 1) * HD]
-            kv_own[KVH + i, block] = values.T.astype(jnp.bfloat16)
+        pairs = dot(normed[:count_rows], wkv_buf[...])
+        for b in range(blocks):
+            rows_b = slice(b * ROWS_Q, (b + 1) * ROWS_Q)
+            for i in range(KVH):
+                kv_own[i, first + b] = pairs[rows_b, i * HD:(i + 1) * HD].astype(jnp.bfloat16)
+                values = pairs[rows_b, (KVH + i) * HD:(KVH + i + 1) * HD]
+                kv_own[KVH + i, first + b] = values.T.astype(jnp.bfloat16)
 
         @pl.when(jnp.logical_not(last))
         def _():
-            kv_copy(block, me + 1).start()
+            kv_copy(chunk, me + 1).start()
+
+        @pl.when(me == 0)
+        def _():
+            kv_twice(chunk).start()
 
         for step in range(STAGES):
-            q_pair = dot(normed[...], wq_buf[:, step * PAIR:(step + 1) * PAIR]).astype(jnp.bfloat16)
+            q_pair = dot(normed[:count_rows], wq_buf[:, step * PAIR:(step + 1) * PAIR]).astype(jnp.bfloat16)
             for half in range(2):
-                queries[2 * step + half, span] = q_pair[:, half * HD:(half + 1) * HD]
+                queries[2 * step + half, first * ROWS_Q:(first + blocks) * ROWS_Q] = q_pair[:, half * HD:(half + 1) * HD]
+
+    def earlier(chunk):
+        @pl.when(me == 0)
+        def _():
+            kv_twice(chunk).wait()
+
+        @pl.when(me > 0)
+        def _():
+            kv_copy(chunk, me - 1).wait_recv()
 
     factor = math.log2(math.e) / math.sqrt(HD)
     sharing = HEADS // KVH
 
-    def keys_of(ref, kv_head):
-        return ref[kv_head].reshape(P_SIZE, HD)
-
-    def values_of(ref, kv_head):
-        return jnp.concatenate([ref[KVH + kv_head, b] for b in range(QUARTERS)], axis=1)
-
-    def own(kv_head, _):
-        keys, values = keys_of(kv_own, kv_head), values_of(kv_own, kv_head)
-        for g in range(sharing):
-            head = kv_head * sharing + g
-            s = dot_t(keys, queries[head])
-            m = jnp.max(s, axis=0, keepdims=True)
-            p = jnp.exp2((s - m) * factor)
-            m_own[head] = m
-            l_own[head] = jnp.sum(p, axis=0, keepdims=True)
-            o_own[head] = dot(values, p.astype(jnp.bfloat16))
-        return 0
-
-    lax.fori_loop(0, KVH, own, 0)
-
-    def out_copy(step):
-        start = step * HD
-        if not isinstance(step, int):
-            start = pl.multiple_of(start, HD)
-        return pltpu.make_async_copy(out_s.at[step], out_hbm.at[0, :, pl.ds(start, HD)], out_sem.at[step])
-
-    @pl.when(me > 0)
-    def _():
-        for block in range(QUARTERS):
-            kv_copy(block, me - 1).wait_recv()
-
-        def earlier(kv_head, _):
-            keys, values = keys_of(kv_prev, kv_head), values_of(kv_prev, kv_head)
-            for g in range(sharing):
-                head = kv_head * sharing + g
-                s = dot_t(keys, queries[head])
-                m = jnp.maximum(jnp.max(s, axis=0, keepdims=True), m_own[head])
-                p = jnp.exp2((s - m) * factor)
-                scale = jnp.exp2((m_own[head] - m) * factor)
-                total = jnp.sum(p, axis=0, keepdims=True) + l_own[head] * scale
-                o = dot(values, p.astype(jnp.bfloat16)) + o_own[head] * scale
-                out_s[head] = (o / total).T.astype(jnp.bfloat16)
-                out_copy(head).start()
+    def attend(pieces):
+        def step(kv_head, _):
+            for q_first, q_blocks, blocks, fresh, final in pieces:
+                columns = slice(q_first * ROWS_Q, (q_first + q_blocks) * ROWS_Q)
+                keys = jnp.concatenate([ref[kv_head, b] for ref, b in blocks], axis=0)
+                values = jnp.concatenate([ref[KVH + kv_head, b] for ref, b in blocks], axis=1)
+                for g in range(sharing):
+                    head = kv_head * sharing + g
+                    s = dot_t(keys, queries[head, columns])
+                    m = jnp.max(s, axis=0, keepdims=True)
+                    if not fresh:
+                        m = jnp.maximum(m, m_run[head, :, columns])
+                    p = jnp.exp2((s - m) * factor)
+                    total = jnp.sum(p, axis=0, keepdims=True)
+                    o = dot(values, p.astype(jnp.bfloat16))
+                    if not fresh:
+                        scale = jnp.exp2((m_run[head, :, columns] - m) * factor)
+                        total = total + l_run[head, :, columns] * scale
+                        o = o + o_run[head, :, columns] * scale
+                    if final:
+                        out = (o / total).T.astype(jnp.bfloat16)
+                        done = 0
+                        for first, chunk_blocks in CHUNKS:
+                            if q_first <= first < q_first + q_blocks:
+                                size = chunk_blocks * ROWS_Q
+                                out_s[head, place(first, chunk_blocks)] = out[done:done + size]
+                                done += size
+                    else:
+                        m_run[head, :, columns] = m
+                        l_run[head, :, columns] = total
+                        o_run[head, :, columns] = o
             return 0
 
-        lax.fori_loop(0, KVH, earlier, 0)
-
-    @pl.when(me == 0)
-    def _():
-        def alone(head, _):
-            out_s[head] = (o_own[head] / l_own[head]).T.astype(jnp.bfloat16)
-            out_copy(head).start()
-            return 0
-
-        lax.fori_loop(0, HEADS, alone, 0)
+        lax.fori_loop(0, KVH, step, 0)
+
+    own = [(kv_own, b) for b in range(QUARTERS)]
+    prev = [(kv_prev, b) for b in range(QUARTERS)]
+    with jax.named_scope("proj0"):
+        project(0)
+    with jax.named_scope("att0"):
+        attend([(0, 2, own[:2], True, False)])
+    with jax.named_scope("proj1"):
+        project(1)
+    with jax.named_scope("ear0"):
+        earlier(0)
+    with jax.named_scope("att1"):
+        attend([(0, 2, own[2:3] + prev[:2], False, False), (2, 1, own[:3] + prev[:2], True, False)])
+    with jax.named_scope("ear1"):
+        earlier(1)
+    with jax.named_scope("att2"):
+        attend([(0, 3, prev[2:3], False, False)])
+    with jax.named_scope("proj2"):
+        project(2)
+    with jax.named_scope("att3"):
+        attend([(3, 1, own + prev[:3], True, False)])
+    with jax.named_scope("ear2"):
+        earlier(2)
+    with jax.named_scope("att4"):
+        attend([(0, 3, own[3:] + prev[3:], False, True), (3, 1, prev[3:], False, True)])
 
     def sent(stage, _):
         for j in peers:
@@ -314,9 +341,16 @@
 
     @pl.when(jnp.logical_not(last))
     def _():
-        for block in range(QUARTERS):
-            kv_copy(block, me + 1).wait_send()
-
+        for chunk in range(len(CHUNKS)):
+            kv_copy(chunk, me + 1).wait_send()
+
+
+def leave(out_s, out_hbm, out_sem):
+    def out_copy(step):
+        return pltpu.make_async_copy(out_s.at[step], out_hbm.at[0, :, pl.ds(step * HD, HD)], out_sem.at[step])
+
+    for step in range(HEADS):
+        out_copy(step).start()
     for step in range(HEADS):
         out_copy(step).wait()
 
@@ -324,18 +358,18 @@
 def body(count, space_time, w_lin, gain_lin, w_query, w_kv, frame_attention_gain):
     rows, width = space_time.shape[1:]
     args = [space_time, w_lin, gain_lin, w_query, w_kv, frame_attention_gain]
-    hbm = pl.BlockSpec(memory_space=pl.ANY)
+    hbm = pl.BlockSpec(memory_space=pltpu.HBM)
     vmem = pl.BlockSpec(memory_space=pltpu.VMEM)
     specs = [hbm, hbm, vmem, hbm, hbm, vmem]
     if count > SB:
         args.append(carried_state(space_time[0], w_lin, count))
         specs.append(vmem)
     bf16, f32 = jnp.bfloat16, jnp.float32
-    return pl.pallas_call(
+    heads = pl.pallas_call(
         functools.partial(kernel, count),
-        out_shape=jax.ShapeDtypeStruct(space_time.shape, bf16),
+        out_shape=pltpu.VMEM((HEADS, P_SIZE, HD), bf16),
         in_specs=specs,
-        out_specs=hbm,
+        out_specs=vmem,
         scratch_shapes=[
             pltpu.VMEM((rows, width), bf16),
             pltpu.VMEM((STAGES, 3, width, PAIR), bf16),
@@ -345,27 +379,34 @@
             pltpu.VMEM((3, rows, PAIR), bf16),
             pltpu.VMEM((STAGES, rows, PAIR), bf16),
             pltpu.VMEM((STAGES, P_SIZE, PAIR), bf16),
-            pltpu.VMEM((ROWS_Q, width), bf16),
+            pltpu.VMEM((2 * ROWS_Q, width), bf16),
             pltpu.VMEM((2 * KVH, QUARTERS, ROWS_Q, HD), bf16),
             pltpu.VMEM((2 * KVH, QUARTERS, ROWS_Q, HD), bf16),
             pltpu.VMEM((HEADS, P_SIZE, HD), bf16),
             pltpu.VMEM((HEADS, HD, P_SIZE), f32),
             pltpu.VMEM((HEADS, 1, P_SIZE), f32),
             pltpu.VMEM((HEADS, 1, P_SIZE), f32),
-            pltpu.VMEM((HEADS, P_SIZE, HD), bf16),
             pltpu.SemaphoreType.DMA((3,)),
             pltpu.SemaphoreType.DMA((STAGES, 3)),
             pltpu.SemaphoreType.DMA((STAGES, SB)),
             pltpu.SemaphoreType.DMA((STAGES, SB)),
-            pltpu.SemaphoreType.DMA((QUARTERS,)),
-            pltpu.SemaphoreType.DMA((QUARTERS,)),
-            pltpu.SemaphoreType.DMA((HEADS,)),
+            pltpu.SemaphoreType.DMA((len(CHUNKS),)),
+            pltpu.SemaphoreType.DMA((len(CHUNKS),)),
         ],
         compiler_params=pltpu.CompilerParams(
             collective_id=0, has_side_effects=True, vmem_limit_bytes=60 * 1024 * 1024
         ),
         name="video_layer",
     )(*args)
+    return pl.pallas_call(
+        leave,
+        out_shape=jax.ShapeDtypeStruct(space_time.shape, bf16),
+        in_specs=[vmem],
+        out_specs=hbm,
+        scratch_shapes=[pltpu.SemaphoreType.DMA((HEADS,))],
+        compiler_params=pltpu.CompilerParams(vmem_limit_bytes=4 * 1024 * 1024),
+        name="leave",
+    )(heads)
 
 
 def solution(mesh):

time: 46.1 us -> 49 us (1.063)
  the two profiles are of different devices: /device:TPU:1 before, /device:TPU:16 now
where the time goes in v1:
time: 49 us; the launch traced here: 48.8 us
  Pallas kernels  48.8 us (100%)
    pallas_call x1, Pallas kernels, body(): pl.pallas_call(functools.partial(kernel, count), out_shape=pltpu.VMEM((HE...  47.8 us
    pallas_call x1, Pallas kernels, body(): pl.pallas_call(leave, out_shape=jax.ShapeDtypeStruct(space_time.shape, bf...  1.03 us

profile of v1, /device:TPU:16, one launch (start us, length us, event | category | flops | bytes accessed | tf_op | source)
XLA Modules:
  0.0 48.8 jit_solution(15785492106314457855)
XLA Ops:
  0.0 47.8 %video_layer.1.out_s = bf16[8,512,128]{2,1,0:T(8,128)(2,1)S(1)} custom-call(bf16[1,512,1024]{2,1,0:T(8,128)(2,1)} %refs_0_.1, bf16[1024,3072]{1,0:T(8,128)(2,1)} %refs_1_.1, bf16[1024]{0:T(1024)(128)(2,1)} %refs_2_.1, bf16[1024,1024]{1,0:T(8,128)(2,1)} %refs_3_.1, bf16[1024,512]{1,0:T(8,128)(2,1)} %refs_4_.1, bf16[1024]{0:T(1024)(128)(2,1)} %refs_5_.1), custom_call_target="tpu_custom_call" | custom-call | tf_op jit(solution)/shard_map/video_layer/pallas_call | solution.py:368
  47.8 1.0 %leave.1 = bf16[1,512,1024]{2,1,0:T(8,128)(2,1)} custom-call(bf16[8,512,128]{2,1,0:T(8,128)(2,1)S(1)} %video_layer.1.out_s), custom_call_target="tpu_custom_call" | custom-call | tf_op jit(solution)/shard_map/leave/pallas_call | solution.py:401

commit v2 on v1

--- a/solution.py
+++ b/solution.py
@@ -19,6 +19,7 @@
 TOKENS = P_SIZE // SB
 QUARTERS = 4
 ROWS_Q = P_SIZE // QUARTERS
+HALF = SB // 2
 CHUNKS = [(0, 2), (2, 1), (3, 1)]
 
 epsilon = 1e-06
@@ -65,7 +66,7 @@
         incoming = refs[0]
         refs = refs[1:]
     (out_s, tokens, w_buf, wq_buf, wkv_buf, gains, qkv, hid, recv, normed, kv_own, kv_prev, queries, o_run, m_run,
-     l_run, in_sem, w_sem, send_sem, recv_sem, kv_send, kv_recv) = refs
+     l_run, extra, in_sem, w_sem, send_sem, recv_sem, kv_send, kv_recv, extra_send, extra_recv) = refs
     width = tokens.shape[1]
     rows = tokens.shape[0]
 
@@ -137,6 +138,15 @@
             device_id={"tm": base + other},
         )
 
+    def extra_piece(stage, k):
+        return pltpu.make_async_remote_copy(
+            src_ref=hid.at[stage, pl.ds((HALF - 1) * TOKENS, TOKENS)],
+            dst_ref=extra.at[stage, pl.ds(pl.multiple_of(k * TOKENS, TOKENS), TOKENS)],
+            send_sem=extra_send.at[stage],
+            recv_sem=extra_recv.at[stage, k],
+            device_id={"tm": base + HALF},
+        )
+
     token_copy.wait()
 
     def mix(stage, _):
@@ -155,15 +165,14 @@
 
         for c in range(3):
             qkv[c] = dot(tokens[...], w_buf[stage, c]).astype(jnp.bfloat16)
-        for half in range(2):
-            columns = slice(half * HD, (half + 1) * HD)
-            if long:
-                state = incoming[2 * stage + half]
-            else:
-                state = jnp.zeros((HD, HD), jnp.float32)
-            gain = gains[stage][:, columns]
-            wide = pl.ds(pl.multiple_of(stage * PAIR + half * HD, HD), HD)
-            for b in range(rows // SPAN):
+        states = [incoming[2 * stage + half] if long else jnp.zeros((HD, HD), jnp.float32) for half in range(2)]
+
+        def spans(numbers):
+            for b, half in [(b, half) for b in numbers for half in range(2)]:
+                columns = slice(half * HD, (half + 1) * HD)
+                state = states[half]
+                gain = gains[stage][:, columns]
+                wide = pl.ds(pl.multiple_of(stage * PAIR + half * HD, HD), HD)
                 span = slice(b * SPAN, (b + 1) * SPAN)
                 q, k, v = qkv[0, span, columns], qkv[1, span, columns], qkv[2, span, columns]
                 local = jnp.where(causal, dot_t(q, k), 0.0).astype(jnp.bfloat16)
@@ -175,10 +184,17 @@
                         jnp.concatenate([state.astype(jnp.bfloat16), v], axis=0),
                     )
                 if b + 1 < rows // SPAN:
-                    state = state + t_dot(k, v)
+                    states[half] = state + t_dot(k, v)
                 mean = jnp.mean(mixed * mixed, axis=-1, keepdims=True)
                 grown = mixed * lax.rsqrt(mean + epsilon) * gain
                 hid[stage, span, columns] = (tokens[span, wide].astype(jnp.float32) + grown).astype(jnp.bfloat16)
+
+        def send(group):
+            for j in group:
+                piece(stage, j).start()
+
+        middle = rows // SPAN // 2
+        spans(range(middle))
 
         @pl.when(stage == 0)
         def _():
@@ -190,8 +206,31 @@
                 )
             pl.semaphore_wait(barrier, SB - 1 + extra)
 
-        for j in near + across[:4] + beside:
-            piece(stage, j).start()
+        @pl.when(jnp.logical_and(bits[3] == 1, stage < STAGES - 1))
+        def _():
+            send(across[:4])
+
+        @pl.when(position > HALF)
+        def _():
+            extra_piece(stage, lax.rem(position, HALF)).start()
+
+        @pl.when(position == HALF)
+        def _():
+            extra[stage, :TOKENS] = hid[stage, (HALF - 1) * TOKENS:HALF * TOKENS]
+
+        @pl.when(bits[3] == 0)
+        def _():
+            send(near + beside)
+
+        spans(range(middle, rows // SPAN))
+
+        @pl.when(bits[3] == 1)
+        def _():
+            send(near + beside)
+
+        @pl.when(jnp.logical_or(bits[3] == 0, stage == STAGES - 1))
+        def _():
+            send(across[:4])
 
         mine = pl.ds(pl.multiple_of(position * TOKENS, TOKENS), TOKENS)
         recv[stage, mine] = hid[stage, mine]
@@ -199,9 +238,20 @@
 
     lax.fori_loop(0, STAGES, mix, 0)
 
-    for j in across[4:]:
-        for stage in range(STAGES):
-            piece(stage, j).start()
+    def whole(j, here, there):
+        return pltpu.make_async_remote_copy(
+            src_ref=hid.at[:, pl.ds(pl.multiple_of(there * TOKENS, TOKENS), TOKENS)],
+            dst_ref=recv.at[:, pl.ds(pl.multiple_of(here * TOKENS, TOKENS), TOKENS)],
+            send_sem=send_sem.at[0, j],
+            recv_sem=recv_sem.at[0, here],
+            device_id={"tm": base + partner(j)},
+        )
+
+    def far(j):
+        whole(j, position, partner(j)).start()
+
+    far(across[4])
+    far(across[5])
 
     def kv_copy(chunk, device):
         first, blocks = CHUNKS[chunk]
@@ -216,6 +266,15 @@
             kv_own.at[:, pl.ds(first, blocks)], kv_prev.at[:, pl.ds(first, blocks)], kv_recv.at[chunk]
         )
 
+    def middle_copy(chunk, device):
+        return pltpu.make_async_remote_copy(
+            src_ref=kv_own.at[:, pl.ds(chunk - 1, 1)], dst_ref=kv_prev.at[:, pl.ds(CHUNKS[chunk][0], 1)],
+            send_sem=kv_send.at[chunk], recv_sem=kv_recv.at[chunk], device_id={"tm": device},
+        )
+
+    passes = jnp.logical_and(jnp.logical_not(last), position != HALF - 1)
+    takes = jnp.logical_and(me > 0, position != HALF)
+
     def place(first, blocks):
         block = sum(lax.rem(bits[i + 2] + ((first >> i) & 1), 2) * (1 << i) for i in range(2))
         block = block // blocks * blocks
@@ -224,15 +283,9 @@
     wkv_copy.wait()
     wq_copy.wait()
 
-    def project(chunk):
-        first, blocks = CHUNKS[chunk]
+    def keys_values(hidden, target, first, blocks):
         count_rows = blocks * ROWS_Q
-        for stage in range(STAGES):
-            for j in range(4 * first, 4 * (first + blocks)):
-                if j:
-                    arrival(stage, j).wait_recv()
-        span = place(first, blocks)
-        parts = [recv[stage, span].astype(jnp.float32) for stage in range(STAGES)]
+        parts = [h.astype(jnp.float32) for h in hidden]
         mean = sum(jnp.sum(p * p, axis=-1, keepdims=True) for p in parts) / width
         inverse = lax.rsqrt(mean + epsilon)
         for stage in range(STAGES):
@@ -243,17 +296,32 @@
         for b in range(blocks):
             rows_b = slice(b * ROWS_Q, (b + 1) * ROWS_Q)
             for i in range(KVH):
-                kv_own[i, first + b] = pairs[rows_b, i * HD:(i + 1) * HD].astype(jnp.bfloat16)
+                target[i, first + b] = pairs[rows_b, i * HD:(i + 1) * HD].astype(jnp.bfloat16)
                 values = pairs[rows_b, (KVH + i) * HD:(KVH + i + 1) * HD]
-                kv_own[KVH + i, first + b] = values.T.astype(jnp.bfloat16)
-
-        @pl.when(jnp.logical_not(last))
+                target[KVH + i, first + b] = values.T.astype(jnp.bfloat16)
+
+    def project(chunk):
+        first, blocks = CHUNKS[chunk]
+        count_rows = blocks * ROWS_Q
+        for j in range(max(4 * first, 1), 4 * (first + blocks)):
+            if j in across[4:]:
+                whole(j, partner(j), position).wait_recv()
+            else:
+                for stage in range(STAGES):
+                    arrival(stage, j).wait_recv()
+        span = place(first, blocks)
+        keys_values([recv[stage, span] for stage in range(STAGES)], kv_own, first, blocks)
+
+        @pl.when(passes)
         def _():
             kv_copy(chunk, me + 1).start()
 
         @pl.when(me == 0)
         def _():
             kv_twice(chunk).start()
+
+        if chunk < 2:
+            far(across[6 + chunk])
 
         for step in range(STAGES):
             q_pair = dot(normed[:count_rows], wq_buf[:, step * PAIR:(step + 1) * PAIR]).astype(jnp.bfloat16)
@@ -265,47 +333,59 @@
         def _():
             kv_twice(chunk).wait()
 
-        @pl.when(me > 0)
+        @pl.when(takes)
         def _():
             kv_copy(chunk, me - 1).wait_recv()
+
+        if chunk:
+            @pl.when(position == HALF)
+            def _():
+                middle_copy(chunk, me - 1).wait_recv()
 
     factor = math.log2(math.e) / math.sqrt(HD)
     sharing = HEADS // KVH
 
     def attend(pieces):
-        def step(kv_head, _):
-            for q_first, q_blocks, blocks, fresh, final in pieces:
-                columns = slice(q_first * ROWS_Q, (q_first + q_blocks) * ROWS_Q)
-                keys = jnp.concatenate([ref[kv_head, b] for ref, b in blocks], axis=0)
-                values = jnp.concatenate([ref[KVH + kv_head, b] for ref, b in blocks], axis=1)
-                for g in range(sharing):
-                    head = kv_head * sharing + g
-                    s = dot_t(keys, queries[head, columns])
-                    m = jnp.max(s, axis=0, keepdims=True)
-                    if not fresh:
-                        m = jnp.maximum(m, m_run[head, :, columns])
-                    p = jnp.exp2((s - m) * factor)
-                    total = jnp.sum(p, axis=0, keepdims=True)
-                    o = dot(values, p.astype(jnp.bfloat16))
-                    if not fresh:
-                        scale = jnp.exp2((m_run[head, :, columns] - m) * factor)
-                        total = total + l_run[head, :, columns] * scale
-                        o = o + o_run[head, :, columns] * scale
-                    if final:
-                        out = (o / total).T.astype(jnp.bfloat16)
-                        done = 0
-                        for first, chunk_blocks in CHUNKS:
-                            if q_first <= first < q_first + q_blocks:
-                                size = chunk_blocks * ROWS_Q
-                                out_s[head, place(first, chunk_blocks)] = out[done:done + size]
-                                done += size
-                    else:
-                        m_run[head, :, columns] = m
-                        l_run[head, :, columns] = total
-                        o_run[head, :, columns] = o
-            return 0
-
-        lax.fori_loop(0, KVH, step, 0)
+        tasks = [(*p, head) for p in pieces for head in range(HEADS)]
+
+        def scores(task):
+            q_first, q_blocks, blocks, _, _, head = task
+            keys = jnp.concatenate([ref[head // sharing, b] for ref, b in blocks], axis=0)
+            return dot_t(keys, queries[head, q_first * ROWS_Q:(q_first + q_blocks) * ROWS_Q])
+
+        def finish(task, s):
+            q_first, q_blocks, blocks, fresh, final, head = task
+            columns = slice(q_first * ROWS_Q, (q_first + q_blocks) * ROWS_Q)
+            values = jnp.concatenate([ref[KVH + head // sharing, b] for ref, b in blocks], axis=1)
+            m = jnp.max(s, axis=0, keepdims=True)
+            if not fresh:
+                m = jnp.maximum(m, m_run[head, :, columns])
+            p = jnp.exp2((s - m) * factor)
+            total = jnp.sum(p, axis=0, keepdims=True)
+            o = dot(values, p.astype(jnp.bfloat16))
+            if not fresh:
+                scale = jnp.exp2((m_run[head, :, columns] - m) * factor)
+                total = total + l_run[head, :, columns] * scale
+                o = o + o_run[head, :, columns] * scale
+            if not final:
+                m_run[head, :, columns] = m
+                l_run[head, :, columns] = total
+                o_run[head, :, columns] = o
+                return
+            out = (o / total).T.astype(jnp.bfloat16)
+            done = 0
+            for first, chunk_blocks in CHUNKS:
+                if q_first <= first < q_first + q_blocks:
+                    size = chunk_blocks * ROWS_Q
+                    out_s[head, place(first, chunk_blocks)] = out[done:done + size]
+                    done += size
+
+        ahead = scores(tasks[0])
+        for t, task in enumerate(tasks):
+            s = ahead
+            if t + 1 < len(tasks):
+                ahead = scores(tasks[t + 1])
+            finish(task, s)
 
     own = [(kv_own, b) for b in range(QUARTERS)]
     prev = [(kv_prev, b) for b in range(QUARTERS)]
@@ -315,34 +395,74 @@
         attend([(0, 2, own[:2], True, False)])
     with jax.named_scope("proj1"):
         project(1)
+
+    @pl.when(position == HALF - 1)
+    def _():
+        for chunk in range(1, len(CHUNKS)):
+            middle_copy(chunk, me + 1).start()
+
+    with jax.named_scope("att1"):
+        attend([(0, 2, own[2:3], False, False), (2, 1, own[:3], True, False)])
+
+    @pl.when(position == HALF)
+    def _():
+        for stage in range(STAGES):
+            for k in range(1, HALF):
+                extra_piece(stage, k).wait_recv()
+        keys_values([extra[stage] for stage in range(STAGES)], kv_prev, 0, 2)
+
     with jax.named_scope("ear0"):
         earlier(0)
-    with jax.named_scope("att1"):
-        attend([(0, 2, own[2:3] + prev[:2], False, False), (2, 1, own[:3] + prev[:2], True, False)])
-    with jax.named_scope("ear1"):
-        earlier(1)
     with jax.named_scope("att2"):
-        attend([(0, 3, prev[2:3], False, False)])
+        attend([(0, 3, prev[:2], False, False)])
+
+    def third():
+        with jax.named_scope("ear1"):
+            earlier(1)
+        with jax.named_scope("att2b"):
+            attend([(0, 3, prev[2:3], False, False)])
+
+    @pl.when(position != HALF)
+    def _():
+        third()
+
     with jax.named_scope("proj2"):
         project(2)
     with jax.named_scope("att3"):
-        attend([(3, 1, own + prev[:3], True, False)])
+        attend([(3, 1, own + prev[:2], True, False)])
+
+    @pl.when(position == HALF)
+    def _():
+        third()
+
     with jax.named_scope("ear2"):
         earlier(2)
     with jax.named_scope("att4"):
-        attend([(0, 3, own[3:] + prev[3:], False, True), (3, 1, prev[3:], False, True)])
+        attend([(0, 3, own[3:] + prev[3:], False, True), (3, 1, prev[2:], False, True)])
 
     def sent(stage, _):
-        for j in peers:
+        for j in across[:4] + near + beside:
             piece(stage, j).wait_send()
         return 0
 
     lax.fori_loop(0, STAGES, sent, 0)
-
-    @pl.when(jnp.logical_not(last))
+    for j in across[4:]:
+        whole(j, position, partner(j)).wait_send()
+
+    for chunk in range(len(CHUNKS)):
+        @pl.when(passes)
+        def _():
+            kv_copy(chunk, me + 1).wait_send()
+
+    @pl.when(position == HALF - 1)
     def _():
-        for chunk in range(len(CHUNKS)):
-            kv_copy(chunk, me + 1).wait_send()
+        for chunk in range(1, len(CHUNKS)):
+            middle_copy(chunk, me + 1).wait_send()
+
+    @pl.when(position > HALF)
+    def _():
+        for stage in range(STAGES):
+            extra_piece(stage, lax.rem(position, HALF)).wait_send()
 
 
 def leave(out_s, out_hbm, out_sem):
@@ -386,12 +506,15 @@
             pltpu.VMEM((HEADS, HD, P_SIZE), f32),
             pltpu.VMEM((HEADS, 1, P_SIZE), f32),
             pltpu.VMEM((HEADS, 1, P_SIZE), f32),
+            pltpu.VMEM((STAGES, HALF * TOKENS, PAIR), bf16),
             pltpu.SemaphoreType.DMA((3,)),
             pltpu.SemaphoreType.DMA((STAGES, 3)),
             pltpu.SemaphoreType.DMA((STAGES, SB)),
             pltpu.SemaphoreType.DMA((STAGES, SB)),
             pltpu.SemaphoreType.DMA((len(CHUNKS),)),
             pltpu.SemaphoreType.DMA((len(CHUNKS),)),
+            pltpu.SemaphoreType.DMA((STAGES,)),
+            pltpu.SemaphoreType.DMA((STAGES, HALF)),
         ],
         compiler_params=pltpu.CompilerParams(
             collective_id=0, has_side_effects=True, vmem_limit_bytes=60 * 1024 * 1024

time: 49 us -> 40.2 us (0.82)
  the two profiles are of different devices: /device:TPU:16 before, /device:TPU:1 now
where the time goes in v2:
time: 40.2 us; the launch traced here: 39.9 us
  Pallas kernels  39.9 us (99%)
    pallas_call x1, Pallas kernels, body(): pl.pallas_call(functools.partial(kernel, count), out_shape=pltpu.VMEM((HE...  38.8 us
    pallas_call x1, Pallas kernels, body(): pl.pallas_call(leave, out_shape=jax.ShapeDtypeStruct(space_time.shape, bf...  1.03 us

profile of v2, /device:TPU:1, one launch (start us, length us, event | category | flops | bytes accessed | tf_op | source)
XLA Modules:
  0.0 39.9 jit_solution(10168299926214451809)
XLA Ops:
  0.0 38.8 %video_layer.1.out_s = bf16[8,512,128]{2,1,0:T(8,128)(2,1)S(1)} custom-call(bf16[1,512,1024]{2,1,0:T(8,128)(2,1)} %refs_0_.1, bf16[1024,3072]{1,0:T(8,128)(2,1)} %refs_1_.1, bf16[1024]{0:T(1024)(128)(2,1)} %refs_2_.1, bf16[1024,1024]{1,0:T(8,128)(2,1)} %refs_3_.1, bf16[1024,512]{1,0:T(8,128)(2,1)} %refs_4_.1, bf16[1024]{0:T(1024)(128)(2,1)} %refs_5_.1), custom_call_target="tpu_custom_call" | custom-call | tf_op jit(solution)/shard_map/video_layer/pallas_call | solution.py:488
  38.8 1.0 %leave.1 = bf16[1,512,1024]{2,1,0:T(8,128)(2,1)} custom-call(bf16[8,512,128]{2,1,0:T(8,128)(2,1)S(1)} %video_layer.1.out_s), custom_call_target="tpu_custom_call" | custom-call | tf_op jit(solution)/shard_map/leave/pallas_call | solution.py:524

commit v3 on v2

--- a/solution.py
+++ b/solution.py
@@ -89,7 +89,7 @@
         if not isinstance(stage, int):
             start = pl.multiple_of(start, PAIR)
         return pltpu.make_async_copy(
-            w_lin_hbm.at[:, pl.ds(start, PAIR)], w_buf.at[stage, c], w_sem.at[stage, c]
+            w_lin_hbm.at[:, pl.ds(start, PAIR)], w_buf.at[stage, c], w_sem.at[stage]
         )
 
     for c in range(3):
@@ -99,6 +99,7 @@
 
     beside, near, across = [1, 2, 3], [4, 5, 6, 7], list(range(8, SB))
     peers = across + near + beside
+    crossing, straight = [10, 11, 14, 15], [8, 9, 12, 13]
     for j in peers:
         pl.semaphore_signal(barrier, inc=1, device_id={"tm": base + partner(j)})
     if long:
@@ -123,35 +124,52 @@
         return pltpu.make_async_remote_copy(
             src_ref=hid.at[stage, pl.ds(pl.multiple_of(other * TOKENS, TOKENS), TOKENS)],
             dst_ref=recv.at[stage, pl.ds(pl.multiple_of(position * TOKENS, TOKENS), TOKENS)],
-            send_sem=send_sem.at[stage, j],
-            recv_sem=recv_sem.at[stage, position],
+            send_sem=send_sem.at[0],
+            recv_sem=recv_sem.at[1 if j in crossing else 0],
             device_id={"tm": base + other},
         )
 
-    def arrival(stage, j):
-        other = partner(j)
-        return pltpu.make_async_remote_copy(
-            src_ref=hid.at[stage, pl.ds(pl.multiple_of(position * TOKENS, TOKENS), TOKENS)],
-            dst_ref=recv.at[stage, pl.ds(pl.multiple_of(other * TOKENS, TOKENS), TOKENS)],
-            send_sem=send_sem.at[stage, j],
-            recv_sem=recv_sem.at[stage, other],
-            device_id={"tm": base + other},
+    def all_of(chunk):
+        first, blocks = CHUNKS[chunk]
+        tokens_in = 4 * blocks * TOKENS - (TOKENS if chunk == 0 else 0)
+        return pltpu.make_async_remote_copy(
+            src_ref=hid.at[:, :tokens_in], dst_ref=recv.at[:, :tokens_in], send_sem=send_sem.at[0],
+            recv_sem=recv_sem.at[chunk], device_id={"tm": base + partner(1)},
+        )
+
+    def all_sent():
+        tokens_out = (SB - 1) * TOKENS
+        return pltpu.make_async_remote_copy(
+            src_ref=hid.at[:, :tokens_out], dst_ref=recv.at[:, :tokens_out], send_sem=send_sem.at[0],
+            recv_sem=recv_sem.at[0], device_id={"tm": base + partner(1)},
+        )
+
+    def all_extra():
+        tokens_in = (HALF - 1) * TOKENS
+        return pltpu.make_async_remote_copy(
+            src_ref=extra.at[:, :tokens_in], dst_ref=extra.at[:, :tokens_in], send_sem=extra_send.at[0],
+            recv_sem=extra_recv.at[0], device_id={"tm": base + partner(1)},
+        )
+
+    def extra_sent():
+        return pltpu.make_async_remote_copy(
+            src_ref=hid.at[:, :TOKENS], dst_ref=recv.at[:, :TOKENS], send_sem=extra_send.at[0],
+            recv_sem=extra_recv.at[0], device_id={"tm": base + partner(1)},
         )
 
     def extra_piece(stage, k):
         return pltpu.make_async_remote_copy(
             src_ref=hid.at[stage, pl.ds((HALF - 1) * TOKENS, TOKENS)],
             dst_ref=extra.at[stage, pl.ds(pl.multiple_of(k * TOKENS, TOKENS), TOKENS)],
-            send_sem=extra_send.at[stage],
-            recv_sem=extra_recv.at[stage, k],
+            send_sem=extra_send.at[0],
+            recv_sem=extra_recv.at[0],
             device_id={"tm": base + HALF},
         )
 
     token_copy.wait()
 
     def mix(stage, _):
-        for c in range(3):
-            w_copy(stage, c).wait()
+        pltpu.make_async_copy(w_buf.at[stage], w_buf.at[stage], w_sem.at[stage]).wait()
 
         @pl.when(stage + 1 < STAGES)
         def _():
@@ -208,7 +226,7 @@
 
         @pl.when(jnp.logical_and(bits[3] == 1, stage < STAGES - 1))
         def _():
-            send(across[:4])
+            send(crossing)
 
         @pl.when(position > HALF)
         def _():
@@ -230,7 +248,7 @@
 
         @pl.when(jnp.logical_or(bits[3] == 0, stage == STAGES - 1))
         def _():
-            send(across[:4])
+            send(crossing)
 
         mine = pl.ds(pl.multiple_of(position * TOKENS, TOKENS), TOKENS)
         recv[stage, mine] = hid[stage, mine]
@@ -242,16 +260,16 @@
         return pltpu.make_async_remote_copy(
             src_ref=hid.at[:, pl.ds(pl.multiple_of(there * TOKENS, TOKENS), TOKENS)],
             dst_ref=recv.at[:, pl.ds(pl.multiple_of(here * TOKENS, TOKENS), TOKENS)],
-            send_sem=send_sem.at[0, j],
-            recv_sem=recv_sem.at[0, here],
+            send_sem=send_sem.at[0],
+            recv_sem=recv_sem.at[2],
             device_id={"tm": base + partner(j)},
         )
 
     def far(j):
         whole(j, position, partner(j)).start()
 
-    far(across[4])
-    far(across[5])
+    for j in straight:
+        far(j)
 
     def kv_copy(chunk, device):
         first, blocks = CHUNKS[chunk]
@@ -276,9 +294,13 @@
     takes = jnp.logical_and(me > 0, position != HALF)
 
     def place(first, blocks):
-        block = sum(lax.rem(bits[i + 2] + ((first >> i) & 1), 2) * (1 << i) for i in range(2))
-        block = block // blocks * blocks
-        return pl.ds(pl.multiple_of(block * ROWS_Q, blocks * ROWS_Q), blocks * ROWS_Q)
+        if blocks == 2:
+            return [pl.ds(pl.multiple_of(2 * bits[3] * ROWS_Q, 2 * ROWS_Q), 2 * ROWS_Q)]
+        row = 1 - bits[1] if first == 2 else bits[1]
+        size = ROWS_Q // 2
+        return [
+            pl.ds(pl.multiple_of((2 * (1 - bits[3]) + plane) * ROWS_Q + row * size, size), size) for plane in range(2)
+        ]
 
     wkv_copy.wait()
     wq_copy.wait()
@@ -303,14 +325,10 @@
     def project(chunk):
         first, blocks = CHUNKS[chunk]
         count_rows = blocks * ROWS_Q
-        for j in range(max(4 * first, 1), 4 * (first + blocks)):
-            if j in across[4:]:
-                whole(j, partner(j), position).wait_recv()
-            else:
-                for stage in range(STAGES):
-                    arrival(stage, j).wait_recv()
-        span = place(first, blocks)
-        keys_values([recv[stage, span] for stage in range(STAGES)], kv_own, first, blocks)
+        all_of(chunk).wait_recv()
+        spans = place(first, blocks)
+        parts = [jnp.concatenate([recv[stage, span] for span in spans], axis=0) for stage in range(STAGES)]
+        keys_values(parts, kv_own, first, blocks)
 
         @pl.when(passes)
         def _():
@@ -319,9 +337,6 @@
         @pl.when(me == 0)
         def _():
             kv_twice(chunk).start()
-
-        if chunk < 2:
-            far(across[6 + chunk])
 
         for step in range(STAGES):
             q_pair = dot(normed[:count_rows], wq_buf[:, step * PAIR:(step + 1) * PAIR]).astype(jnp.bfloat16)
@@ -376,9 +391,9 @@
             done = 0
             for first, chunk_blocks in CHUNKS:
                 if q_first <= first < q_first + q_blocks:
-                    size = chunk_blocks * ROWS_Q
-                    out_s[head, place(first, chunk_blocks)] = out[done:done + size]
-                    done += size
+                    for span in place(first, chunk_blocks):
+                        out_s[head, span] = out[done:done + span.size]
+                        done += span.size
 
         ahead = scores(tasks[0])
         for t, task in enumerate(tasks):
@@ -406,9 +421,7 @@
 
     @pl.when(position == HALF)
     def _():
-        for stage in range(STAGES):
-            for k in range(1, HALF):
-                extra_piece(stage, k).wait_recv()
+        all_extra().wait_recv()
         keys_values([extra[stage] for stage in range(STAGES)], kv_prev, 0, 2)
 
     with jax.named_scope("ear0"):
@@ -440,14 +453,7 @@
     with jax.named_scope("att4"):
         attend([(0, 3, own[3:] + prev[3:], False, True), (3, 1, prev[2:], False, True)])
 
-    def sent(stage, _):
-        for j in across[:4] + near + beside:
-            piece(stage, j).wait_send()
-        return 0
-
-    lax.fori_loop(0, STAGES, sent, 0)
-    for j in across[4:]:
-        whole(j, position, partner(j)).wait_send()
+    all_sent().wait_send()
 
     for chunk in range(len(CHUNKS)):
         @pl.when(passes)
@@ -461,8 +467,7 @@
 
     @pl.when(position > HALF)
     def _():
-        for stage in range(STAGES):
-            extra_piece(stage, lax.rem(position, HALF)).wait_send()
+        extra_sent().wait_send()
 
 
 def leave(out_s, out_hbm, out_sem):
@@ -508,13 +513,13 @@
             pltpu.VMEM((HEADS, 1, P_SIZE), f32),
             pltpu.VMEM((STAGES, HALF * TOKENS, PAIR), bf16),
             pltpu.SemaphoreType.DMA((3,)),
-            pltpu.SemaphoreType.DMA((STAGES, 3)),
-            pltpu.SemaphoreType.DMA((STAGES, SB)),
-            pltpu.SemaphoreType.DMA((STAGES, SB)),
+            pltpu.SemaphoreType.DMA((STAGES,)),
+            pltpu.SemaphoreType.DMA((1,)),
             pltpu.SemaphoreType.DMA((len(CHUNKS),)),
             pltpu.SemaphoreType.DMA((len(CHUNKS),)),
-            pltpu.SemaphoreType.DMA((STAGES,)),
-            pltpu.SemaphoreType.DMA((STAGES, HALF)),
+            pltpu.SemaphoreType.DMA((len(CHUNKS),)),
+            pltpu.SemaphoreType.DMA((1,)),
+            pltpu.SemaphoreType.DMA((1,)),
         ],
         compiler_params=pltpu.CompilerParams(
             collective_id=0, has_side_effects=True, vmem_limit_bytes=60 * 1024 * 1024

time: 40.2 us -> 38.4 us (0.955)
  the two profiles are of different devices: /device:TPU:1 before, /device:TPU:24 now
where the time goes in v3:
time: 38.4 us; the launch traced here: 38.2 us
  Pallas kernels  38.2 us (99%)
    pallas_call x1, Pallas kernels, body(): pl.pallas_call(functools.partial(kernel, count), out_shape=pltpu.VMEM((HE...  37.2 us
    pallas_call x1, Pallas kernels, body(): pl.pallas_call(leave, out_shape=jax.ShapeDtypeStruct(space_time.shape, bf...  1.03 us

profile of v3, /device:TPU:24, one launch (start us, length us, event | category | flops | bytes accessed | tf_op | source)
XLA Modules:
  0.0 38.2 jit_solution(13095559835398233847)
XLA Ops:
  0.0 37.2 %video_layer.1.out_s = bf16[8,512,128]{2,1,0:T(8,128)(2,1)S(1)} custom-call(bf16[1,512,1024]{2,1,0:T(8,128)(2,1)} %refs_0_.1, bf16[1024,3072]{1,0:T(8,128)(2,1)} %refs_1_.1, bf16[1024]{0:T(1024)(128)(2,1)} %refs_2_.1, bf16[1024,1024]{1,0:T(8,128)(2,1)} %refs_3_.1, bf16[1024,512]{1,0:T(8,128)(2,1)} %refs_4_.1, bf16[1024]{0:T(1024)(128)(2,1)} %refs_5_.1), custom_call_target="tpu_custom_call" | custom-call | tf_op jit(solution)/shard_map/video_layer/pallas_call | solution.py:493
  37.2 1.0 %leave.1 = bf16[1,512,1024]{2,1,0:T(8,128)(2,1)} custom-call(bf16[8,512,128]{2,1,0:T(8,128)(2,1)S(1)} %video_layer.1.out_s), custom_call_target="tpu_custom_call" | custom-call | tf_op jit(solution)/shard_map/leave/pallas_call | solution.py:529
